TPU v7x, 256 devices: a whole 4x4x8 slice. The times are simulated.
256 devices in a mesh: seq: 32 (over y_lo, z, core), head: 8 (over y_hi, x).
Axes of the slice: x: 4, y: 4 (y_hi: 2, y_lo: 2; y = y_hi * 2 + y_lo), z: 8, core: 2. Of those that a mesh axis runs over, the one named last changes fastest.
Arguments:
- inputs: bfloat16 [16384, 5376], P('seq'), may hold values from -6 to 6
- queries: bfloat16 [16384, 4096], P('seq', 'head'), may hold values from -6 to 6
- key_matrix: bfloat16 [5376, 2048], P('seq', 'head'), may hold values from -0.078125 to 0.078125
- value_matrix: bfloat16 [5376, 2048], P('seq', 'head'), may hold values from -0.078125 to 0.078125
- readout: bfloat16 [4096, 512], P('head'), may hold values from -6 to 6
- token_mask: int32 [16384], P('seq'), may hold values 0 or 1
- targets: int32 [16384], P('seq'), may hold values from 0 to 511
Outputs:
- query_grad: float32 [16384, 4096], P('seq', 'head')
- input_grad: float32 [16384, 5376], P('seq', 'head')
All inputs are finite; a program needn't handle non-finite values. No bound on the sum of `token_mask` on one device may be relied on, other than what follows from the above.
Results may differ from a plain program's by a relative error of at most 0.028.
Values may be sent and summed in bfloat16 or wider, within the bound.
No kernel may reach another device: no remote copies, remote signals or barrier semaphores. Data moves between devices by JAX's collectives and lax.ppermute only.
A program may use at most 128 MiB of HBM per device.

v0:
```python
import jax
import jax.numpy as jnp
from jax import lax
from jax.sharding import PartitionSpec as P

HEAD_SIZE = 128
WINDOW_KEYS = 1024
norm_eps = 1e-06
softcap = 30.0
score_scale = 168.0 ** (-0.5)


def passed_along(value, axis, steps):
    count = lax.axis_size(axis)
    leading, last = (max(0, -steps), min(count, count - steps))
    return lax.ppermute(value, axis, [(source, source + steps) for source in range(leading, last)])


def normalized_rows(value_rows):
    inverse = lax.rsqrt(jnp.mean(value_rows * value_rows, axis=-1, keepdims=True) + norm_eps)
    return (value_rows * inverse, inverse)


def unit_norm_backward(unit, inverse, upstream):
    return inverse * (upstream - unit * jnp.mean(unit * upstream, axis=-1, keepdims=True))


def shards(inputs, queries, key_matrix, value_matrix, readout, token_mask, targets):
    tokens = inputs.shape[0]
    kv_width = key_matrix.shape[1]
    kv_heads = kv_width // HEAD_SIZE
    q_heads = queries.shape[1] // HEAD_SIZE
    query_groups = q_heads // kv_heads
    reach = WINDOW_KEYS // tokens
    span = (reach + 1) * tokens
    stacked = jnp.concatenate([key_matrix, value_matrix], axis=1)
    full_weight = lax.all_gather(stacked, "seq", axis=0, tiled=True)
    projected = jnp.dot(inputs, full_weight, preferred_element_type=jnp.float32)
    key_unscaled = projected[:, :kv_width].reshape(tokens, kv_heads, HEAD_SIZE)
    value_rows = projected[:, kv_width:].astype(jnp.bfloat16).reshape(tokens, kv_heads, HEAD_SIZE)
    key_unit_rows, key_inverse_norm = normalized_rows(key_unscaled)
    key_normalized_rows = key_unit_rows.astype(jnp.bfloat16)
    query_unit_rows, query_inverse_norm = normalized_rows(
        queries.astype(jnp.float32).reshape(tokens, kv_heads, query_groups, HEAD_SIZE)
    )
    query_hat = query_unit_rows.astype(jnp.bfloat16)
    paired = jnp.concatenate([key_normalized_rows, value_rows], axis=-1)
    earlier = [passed_along(paired, "seq", offset) for offset in range(reach, 0, -1)]
    window_kv = jnp.concatenate(earlier + [paired], axis=0)
    key_block = window_kv[..., :HEAD_SIZE]
    value_block = window_kv[..., HEAD_SIZE:]
    first = lax.axis_index("seq") * tokens
    query_pos = first + jnp.arange(tokens, dtype=jnp.int32)
    key_pos = first - reach * tokens + jnp.arange(span, dtype=jnp.int32)
    distance = query_pos[:, None] - key_pos[None, :]
    visible = (distance >= 0) & (distance < WINDOW_KEYS) & (key_pos[None, :] >= 0)
    scores = (
        jnp.einsum("qkgd,jkd->kgqj", query_hat, key_block, preferred_element_type=jnp.float32)
        * score_scale
    )
    raised = jnp.where(visible, jnp.exp(scores), 0.0)
    attn = (raised / jnp.sum(raised, axis=-1, keepdims=True)).astype(jnp.bfloat16)
    attended = jnp.einsum(
        "kgqj,jkd->qkgd", attn, value_block, preferred_element_type=jnp.float32
    ).astype(jnp.bfloat16)
    flat = attended.reshape(tokens, q_heads * HEAD_SIZE)
    partial_value = jnp.dot(flat, readout, preferred_element_type=jnp.float32)
    logits = lax.psum(partial_value.astype(jnp.bfloat16), "head").astype(jnp.float32)
    capped = softcap * jnp.tanh(logits / softcap)
    expo = jnp.exp(capped)
    probs = expo / jnp.sum(expo, axis=-1, keepdims=True)
    onehot = (targets[:, None] == jnp.arange(logits.shape[1], dtype=jnp.int32)[None, :]).astype(
        jnp.float32
    )
    chosen = token_mask.astype(jnp.float32)[:, None]
    dlogits = (chosen * (probs - onehot) * (1.0 - (capped / softcap) ** 2)).astype(jnp.bfloat16)
    attended_grad = lax.dot_general(
        dlogits, readout, (((1,), (1,)), ((), ())), preferred_element_type=jnp.float32
    )
    attended_grad = attended_grad.astype(jnp.bfloat16).reshape(
        tokens, kv_heads, query_groups, HEAD_SIZE
    )
    d_weights = jnp.einsum(
        "qkgd,jkd->kgqj", attended_grad, value_block, preferred_element_type=jnp.float32
    )
    attn_f = attn.astype(jnp.float32)
    d_scores = (attn_f * (d_weights - jnp.sum(attn_f * d_weights, axis=-1, keepdims=True))).astype(
        jnp.bfloat16
    )
    d_query_hat = (
        jnp.einsum("kgqj,jkd->qkgd", d_scores, key_block, preferred_element_type=jnp.float32)
        * score_scale
    )
    d_key_hat = (
        jnp.einsum("kgqj,qkgd->jkd", d_scores, query_hat, preferred_element_type=jnp.float32)
        * score_scale
    )
    d_value = jnp.einsum("kgqj,qkgd->jkd", attn, attended_grad, preferred_element_type=jnp.float32)
    query_grad = unit_norm_backward(query_unit_rows, query_inverse_norm, d_query_hat).reshape(
        tokens, q_heads * HEAD_SIZE
    )
    pieces_all = jnp.concatenate([d_key_hat, d_value], axis=-1)
    pieces = [
        pieces_all[slot_index * tokens : (slot_index + 1) * tokens]
        for slot_index in range(reach + 1)
    ]
    total = pieces[reach]
    for offset in range(1, reach + 1):
        total = total + passed_along(
            pieces[reach - offset].astype(jnp.bfloat16), "seq", -offset
        ).astype(jnp.float32)
    key_weight_gradient = (
        unit_norm_backward(key_unit_rows, key_inverse_norm, total[..., :HEAD_SIZE])
        .astype(jnp.bfloat16)
        .reshape(tokens, kv_width)
    )
    value_weight_gradient = total[..., HEAD_SIZE:].astype(jnp.bfloat16).reshape(tokens, kv_width)
    both_grad = jnp.concatenate([key_weight_gradient, value_weight_gradient], axis=1)
    partial_grad = lax.dot_general(
        both_grad, full_weight, (((1,), (1,)), ((), ())), preferred_element_type=jnp.float32
    )
    input_grad = lax.psum_scatter(
        partial_grad.astype(jnp.bfloat16), "head", scatter_dimension=1, tiled=True
    ).astype(jnp.float32)
    return (query_grad, input_grad)


def solution(mesh):
    in_specs = (
        P("seq", None),
        P("seq", "head"),
        P("seq", "head"),
        P("seq", "head"),
        P("head", None),
        P("seq"),
        P("seq"),
    )
    out_specs = (P("seq", "head"), P("seq", "head"))
    return jax.shard_map(shards, mesh=mesh, in_specs=in_specs, out_specs=out_specs, check_vma=False)
```

profile of v0, /device:TPU:1, one launch (start us, length us, event | category | flops | bytes accessed | tf_op | source)
XLA Modules:
  0.0 374.4 jit_solution(5601554933877116850)
XLA Ops:
  7.2 1.7 pad_maximum_fusion.2
  10.4 72.4 %all-gather.2.cloned.1.call-done = bf16[5376,512]{1,0:T(8,128)(2,1)} async-done(((bf16[168,512]{1,0:T(8,128)(2,1)}), bf16[5376,512]{1,0:T(8,128)(2,1)}) %all-gather.2.cloned.1.call-update) | async-done | bytes 5505040 | tf_op jit(solution)/shard_map/all_gather | solution.py:37
  82.8 6.8 %convolution_bitcast_fusion.2 = f32[512,512]{0,1:T(8,128)S(1)} fusion(bf16[5376,512]{1,0:T(8,128)(2,1)} %all-gather.2.cloned.1.call-done, bf16[512,5376]{1,0:T(8,128)(2,1)} %param.7), kind=kOutput, calls=%fused_computation.24 | convolution fusion | flops 2818572288 | bytes 12058624 | tf_op jit(solution)/shard_map/dot_general | solution.py:38
  90.4 2.4 collective-permute-start.1
  92.8 3.8 %collective-permute-start = (bf16[512,2,256]{2,0,1:T(8,128)(2,1)S(1)}, bf16[512,2,256]{2,0,1:T(8,128)(2,1)S(1)}, u32[]{:S(2)}, u32[]{:S(2)}) collective-permute-start(bf16[512,2,256]{2,0,1:T(8,128)(2,1)S(1)} %pad_maximum_fusion.1), channel_id=1, source_target_pairs={{0,16},{8,24},{16,32},{24,40},{32,48},{40,56},{48,64},{56,72},{64,... | collective-permute-start | bytes 1572872 | tf_op jit(solution)/shard_map/ppermute | solution.py:16
  97.9 3.9 %collective-permute-done.1 = bf16[512,2,256]{2,0,1:T(8,128)(2,1)S(1)} collective-permute-done((bf16[512,2,256]{2,0,1:T(8,128)(2,1)S(1)}, bf16[512,2,256]{2,0,1:T(8,128)(2,1)S(1)}, u32[]{:S(2)}, u32[]{:S(2)}) %collective-permute-start.1) | collective-permute-done | bytes 524320 | tf_op jit(solution)/shard_map/ppermute | solution.py:16
  101.8 8.3 %collective-permute-done = bf16[512,2,256]{2,0,1:T(8,128)(2,1)S(1)} collective-permute-done((bf16[512,2,256]{2,0,1:T(8,128)(2,1)S(1)}, bf16[512,2,256]{2,0,1:T(8,128)(2,1)S(1)}, u32[]{:S(2)}, u32[]{:S(2)}) %collective-permute-start) | collective-permute-done | bytes 524320 | tf_op jit(solution)/shard_map/ppermute | solution.py:16
  110.3 3.3 fusion.2
  113.6 2.7 divide_convert_fusion
  116.3 1.8 copy-done.5
  118.1 2.6 copy-done.2
  123.3 87.0 %all-reduce.2.cloned.1.call-done = bf16[512,512]{1,0:T(8,128)(2,1)} async-done(((bf16[512,512]{1,0:T(8,128)(2,1)}), bf16[512,512]{1,0:T(8,128)(2,1)}) %all-reduce.2.cloned.1.call-update) | async-done | bytes 524304 | tf_op jit(solution)/shard_map/psum | solution.py:68
  211.9 2.3 convolution_convert_fusion.1
  214.2 1.8 convolution_bitcast_fusion
  216.1 6.9 %fusion = (f32[2,2,512]{2,1,0:T(2,128)S(1)}, f32[2,1536,512,2]{2,1,3,0:T(8,128)}) fusion(bf16[2,2,512,1536]{2,3,1,0:T(8,128)(2,1)S(1)} %copy-done.3, bf16[512,2,2,128]{0,3,2,1:T(8,128)(2,1)S(1)} %bitcast.87, bf16[1536,2,256]{2,0,1:T(8,128)(2,1)S(1)} %maximum_maximum_fusion), kind=kOutput, calls=%fused_computation.2 | convolution fusion | flops 814741504 | bytes 20193280 | tf_op jit(solution)/shard_map/qkgd,jkd->kgqj/dot_general | solution.py:83
  223.0 6.9 %fusion.1 = bf16[2,2,512,1536]{2,3,1,0:T(8,128)(2,1)S(1)} fusion(f32[2,1536,512,2]{2,1,3,0:T(8,128)} %get-tuple-element.11, f32[2,2,512]{2,1,0:T(2,128)S(1)} %get-tuple-element.10, f32[2,2,512]{2,1,0:T(2,128)S(1)} %get-tuple-element.8, f32[2,1536,512,2]{2,1,3,0:T(8,128)S(1)} %bitcast.85, pred[512,1536]{0,1:T(8,128)(4,1)S(1)} %copy-done.9), kind=kLoop, calls=%fused_computation.3 | loop fusion | flops 25165824 | bytes 32260096 | tf_op jit(solution)/shard_map/convert_element_type | solution.py:87
  229.9 1.8 fusion.7
  232.8 8.3 %collective-permute-start.2 = (bf16[512,2,256]{2,0,1:T(8,128)(2,1)S(1)}, bf16[512,2,256]{2,0,1:T(8,128)(2,1)S(1)}, u32[]{:S(2)}, u32[]{:S(2)}) collective-permute-start(bf16[512,2,256]{2,0,1:T(8,128)(2,1)S(1)} %get-tuple-element.6), channel_id=1, source_target_pairs={{8,0},{16,8},{24,16},{32,24},{40,32},{48,40},{56,48},{64,56},{72,6... | collective-permute-start | bytes 1572872 | tf_op jit(solution)/shard_map/ppermute | solution.py:16
  242.4 10.4 %collective-permute-done.2 = bf16[512,2,256]{2,0,1:T(8,128)(2,1)S(1)} collective-permute-done((bf16[512,2,256]{2,0,1:T(8,128)(2,1)S(1)}, bf16[512,2,256]{2,0,1:T(8,128)(2,1)S(1)}, u32[]{:S(2)}, u32[]{:S(2)}) %collective-permute-start.2) | collective-permute-done | bytes 524320 | tf_op jit(solution)/shard_map/ppermute | solution.py:16
  252.8 4.1 %collective-permute-done.3 = bf16[512,2,256]{2,0,1:T(8,128)(2,1)S(1)} collective-permute-done((bf16[512,2,256]{2,0,1:T(8,128)(2,1)S(1)}, bf16[512,2,256]{2,0,1:T(8,128)(2,1)S(1)}, u32[]{:S(2)}, u32[]{:S(2)}) %collective-permute-start.3) | collective-permute-done | bytes 524320 | tf_op jit(solution)/shard_map/ppermute | solution.py:16
  259.8 7.4 %convolution_convert_fusion = bf16[512,5376]{0,1:T(8,128)(2,1)} fusion(bf16[5376,512]{1,0:T(8,128)(2,1)} %all-gather.2.cloned.1.call-done, bf16[512,256]{0,1:T(8,128)(2,1)S(1)} %bitcast.92, bf16[512,256]{0,1:T(8,128)(2,1)S(1)} %bitcast.93), kind=kOutput, calls=%fused_computation.8 | convolution fusion | flops 2822373376 | bytes 11534336 | tf_op jit(solution)/shard_map/dot_general | solution.py:119
  267.3 3.9 %multiply_reduce_fusion = (f32[512,2,2]{0,2,1:T(2,128)S(1)}, f32[512,2,2,128]{0,3,2,1:T(8,128)S(1)}) fusion(f32[512,512]{0,1:T(8,128)S(1)} %copy.23, f32[512,2,2]{0,2,1:T(2,128)S(1)} %add_rsqrt_fusion, bf16[2,2,512,1536]{2,3,1,0:T(8,128)(2,1)} %copy-done.4, bf16[1536,2,256]{2,0,1:T(8,128)(2,1)S(1)} %maximum_maximum_fusion), kind=kOutput, calls=%fused_computation.32 | convolution fusion | flops 806352896 | bytes 9191424 | tf_op jit(solution)/shard_map/kgqj,jkd->qkgd/dot_general | solution.py:91
  272.8 92.7 %reduce-scatter.2.cloned.1.call-done = bf16[512,672]{0,1:T(8,128)(2,1)} async-done(((bf16[512,5376]{0,1:T(8,128)(2,1)}), bf16[512,672]{0,1:T(8,128)(2,1)}) %reduce-scatter.2.cloned.1.call-update) | async-done | bytes 688144 | tf_op jit(solution)/shard_map/reduce_scatter | solution.py:122
  365.5 2.4 convert_element_type.76
  (68 shorter events, 14.6 us)
Async XLA Ops:
  7.2 114.6 %copy-start = (bf16[512,512]{1,0:T(8,128)(2,1)S(1)}, bf16[512,512]{1,0:T(8,128)(2,1)}, u32[]{:S(2)}) copy-start(bf16[512,512]{1,0:T(8,128)(2,1)} %param.11) | copy-start | bytes 1572868
  7.2 75.6 %all-gather.2.cloned.1.call-start = ((), (), s32[]{:S(2)}) async-start(), calls=%async_computation.1 | async-start | bytes 5677056 | tf_op jit(solution)/shard_map/all_gather | solution.py:37
  8.9 201.4 %all-reduce.2.cloned.1.call-start = ((), (), s32[]{:S(2)}) async-start(), calls=%async_computation.2 | async-start | bytes 1048576 | tf_op jit(solution)/shard_map/psum | solution.py:68
  90.0 11.9 %copy-start.6 = (f32[512,2,128]{2,0,1:T(8,128)}, f32[512,2,128]{2,0,1:T(8,128)S(1)}, u32[]{:S(2)}) copy-start(f32[512,2,128]{2,0,1:T(8,128)S(1)} %copy.24) | copy-start | bytes 1572868
  90.4 11.4 %collective-permute-start.1 = (bf16[512,2,256]{2,0,1:T(8,128)(2,1)S(1)}, bf16[512,2,256]{2,0,1:T(8,128)(2,1)S(1)}, u32[]{:S(2)}, u32[]{:S(2)}) collective-permute-start(bf16[512,2,256]{2,0,1:T(8,128)(2,1)S(1)} %pad_maximum_fusion.1), channel_id=1, source_target_pairs={{0,8},{8,16},{16,24},{24,32},{32,40},{40,48},{48,56},{56,64},{64,7... | collective-permute-start | bytes 1572872 | tf_op jit(solution)/shard_map/ppermute | solution.py:16
  92.8 17.3 %collective-permute-start = (bf16[512,2,256]{2,0,1:T(8,128)(2,1)S(1)}, bf16[512,2,256]{2,0,1:T(8,128)(2,1)S(1)}, u32[]{:S(2)}, u32[]{:S(2)}) collective-permute-start(bf16[512,2,256]{2,0,1:T(8,128)(2,1)S(1)} %pad_maximum_fusion.1), channel_id=1, source_target_pairs={{0,16},{8,24},{16,32},{24,40},{32,48},{40,56},{48,64},{56,72},{64,... | collective-permute-start | bytes 1572872 | tf_op jit(solution)/shard_map/ppermute | solution.py:16
  97.9 15.7 %copy-start.8 = (pred[512,1536]{0,1:T(8,128)(4,1)}, pred[512,1536]{0,1:T(8,128)(4,1)S(1)}, u32[]{:S(2)}) copy-start(pred[512,1536]{0,1:T(8,128)(4,1)S(1)} %fusion.5) | copy-start | bytes 2359300
  113.6 4.5 %copy-start.5 = (f32[2,1536,512,2]{2,1,3,0:T(8,128)}, f32[2,1536,512,2]{2,1,3,0:T(8,128)S(1)}, u32[]{:S(2)}) copy-start(f32[2,1536,512,2]{2,1,3,0:T(8,128)S(1)} %get-tuple-element.9) | copy-start | bytes 37748740
  118.1 2.6 copy-start.2
  120.7 2.6 copy-start.10
  120.7 91.2 %copy-start.11 = (s32[512]{0:T(512)S(1)}, s32[512]{0:T(512)}, u32[]{:S(2)}) copy-start(s32[512]{0:T(512)} %param.13) | copy-start | bytes 6148
  123.1 242.4 %reduce-scatter.2.cloned.1.call-start = ((), (), s32[]{:S(2)}) async-start(), calls=%async_computation.3 | async-start | bytes 6193152 | tf_op jit(solution)/shard_map/reduce_scatter | solution.py:122
  210.3 3.9 %copy-start.3 = (bf16[2,2,512,1536]{2,3,1,0:T(8,128)(2,1)S(1)}, bf16[2,2,512,1536]{2,3,1,0:T(8,128)(2,1)}, u32[]{:S(2)}) copy-start(bf16[2,2,512,1536]{2,3,1,0:T(8,128)(2,1)} %copy-done.2) | copy-start | bytes 18874372
  214.2 8.7 %slice-start = ((s8[12582912]{0:T(1024)(128)(4,1)}), s8[4194304]{0:T(1024)(128)(4,1)S(1)}, s32[]{:S(2)}) async-start(s8[12582912]{0:T(1024)(128)(4,1)} %bitcast.84), calls=%async_computation.4 | async-start | bytes 8388608
  216.0 6.9 %slice-start.1 = ((s8[12582912]{0:T(1024)(128)(4,1)}), s8[4194304]{0:T(1024)(128)(4,1)S(1)}, s32[]{:S(2)}) async-start(s8[12582912]{0:T(1024)(128)(4,1)} %bitcast.84), calls=%async_computation.5 | async-start | bytes 8388608
  216.1 6.9 %slice-start.2 = ((s8[12582912]{0:T(1024)(128)(4,1)}), s8[4194304]{0:T(1024)(128)(4,1)S(1)}, s32[]{:S(2)}) async-start(s8[12582912]{0:T(1024)(128)(4,1)} %bitcast.84), calls=%async_computation.6 | async-start | bytes 8388608
  216.1 6.9 %copy-start.9 = (pred[512,1536]{0,1:T(8,128)(4,1)S(1)}, pred[512,1536]{0,1:T(8,128)(4,1)}, u32[]{:S(2)}) copy-start(pred[512,1536]{0,1:T(8,128)(4,1)} %copy-done.8) | copy-start | bytes 2359300
  229.9 2.7 copy-start.4
  232.6 24.6 %copy-start.7 = (f32[512,2,128]{2,0,1:T(8,128)S(1)}, f32[512,2,128]{2,0,1:T(8,128)}, u32[]{:S(2)}) copy-start(f32[512,2,128]{2,0,1:T(8,128)} %copy-done.6) | copy-start | bytes 1572868
  232.8 20.0 %collective-permute-start.2 = (bf16[512,2,256]{2,0,1:T(8,128)(2,1)S(1)}, bf16[512,2,256]{2,0,1:T(8,128)(2,1)S(1)}, u32[]{:S(2)}, u32[]{:S(2)}) collective-permute-start(bf16[512,2,256]{2,0,1:T(8,128)(2,1)S(1)} %get-tuple-element.6), channel_id=1, source_target_pairs={{8,0},{16,8},{24,16},{32,24},{40,32},{48,40},{56,48},{64,56},{72,6... | collective-permute-start | bytes 1572872 | tf_op jit(solution)/shard_map/ppermute | solution.py:16
  241.1 15.8 %collective-permute-start.3 = (bf16[512,2,256]{2,0,1:T(8,128)(2,1)S(1)}, bf16[512,2,256]{2,0,1:T(8,128)(2,1)S(1)}, u32[]{:S(2)}, u32[]{:S(2)}) collective-permute-start(bf16[512,2,256]{2,0,1:T(8,128)(2,1)S(1)} %get-tuple-element.7), channel_id=1, source_target_pairs={{16,0},{24,8},{32,16},{40,24},{48,32},{56,40},{64,48},{72,56},{80,... | collective-permute-start | bytes 1572872 | tf_op jit(solution)/shard_map/ppermute | solution.py:16
  267.2 100.6 %copy-start.1 = (bf16[512,512]{1,0:T(8,128)(2,1)S(1)}, bf16[512,512]{1,0:T(8,128)(2,1)}, u32[]{:S(2)}) copy-start(bf16[512,512]{1,0:T(8,128)(2,1)} %param.11) | copy-start | bytes 1572868
Sparse Core Ops, SparseCore 0:
  10.4 72.3 all-gather.1
  123.2 87.0 all-reduce.1
  267.4 98.0 reduce-scatter.1
where the time goes:
time: 375 us; the launch traced here: 374 us
  waiting for transfers between devices  279 us (74%)
  matrix products  36.5 us (10%)
  other arithmetic  18.3 us (5%)
  starting transfers between devices  16.1 us (4%)
  between operations  14.2 us (4%)
  local copies, waits for them, and re-layouts  10.4 us (3%)
    reduce_scatter x1, waiting for transfers between devices, shards(): lax.psum_scatter(partial_grad.astype(jnp.bfloat16), 'head', scatter_dimen...  92.7 us
    psum x1, waiting for transfers between devices, shards(): lax.psum(partial_value.astype(jnp.bfloat16), 'head').astype(jnp.float32)  87 us
    all_gather x1, waiting for transfers between devices, shards(): full_weight = lax.all_gather(stacked, 'seq', axis=0, tiled=True)  72.4 us
    ppermute x4, waiting for transfers between devices, passed_along(): lax.ppermute(value, axis, [(source, source + steps) for source in range(l...  26.8 us
    ppermute x4, starting transfers between devices, passed_along(): lax.ppermute(value, axis, [(source, source + steps) for source in range(l...  15.8 us
  transfers between devices with their start and end apart: 7, of which 7 were waited for; matrix products, arithmetic and copies ran while one was open for 2% of the time, Pallas kernels for 0%

commit v1 on v0

--- a/solution.py
+++ b/solution.py
@@ -34,7 +34,9 @@
     reach = WINDOW_KEYS // tokens
     span = (reach + 1) * tokens
     stacked = jnp.concatenate([key_matrix, value_matrix], axis=1)
-    full_weight = lax.all_gather(stacked, "seq", axis=0, tiled=True)
+    full_weight = jnp.concatenate(
+        lax.all_to_all(jnp.stack([stacked] * lax.axis_size("seq")), "seq", 0, 0), axis=0
+    )
     projected = jnp.dot(inputs, full_weight, preferred_element_type=jnp.float32)
     key_unscaled = projected[:, :kv_width].reshape(tokens, kv_heads, HEAD_SIZE)
     value_rows = projected[:, kv_width:].astype(jnp.bfloat16).reshape(tokens, kv_heads, HEAD_SIZE)

time: 375 us -> 439 us (1.17)
  waiting for transfers between devices: 279 us -> 331 us
  starting transfers between devices: 16.1 us -> 25.3 us
    all_to_all x0 -> x1, waiting for transfers between devices: none -> 122 us  [shards(): lax.all_to_all(jnp.stack([stacked] * lax.axis_size('seq')), 'seq', 0, 0)]
    all_gather x1 -> x0, waiting for transfers between devices: 72.4 us -> none  [shards(): full_weight = lax.all_gather(stacked, 'seq', axis=0, tiled=True)]
    all_to_all x0 -> x1, starting transfers between devices: none -> 11.3 us  [shards(): lax.all_to_all(jnp.stack([stacked] * lax.axis_size('seq')), 'seq', 0, 0)]
where the time goes in v1:
time: 439 us
  waiting for transfers between devices  331 us (75%)
  matrix products  36.5 us (8%)
  starting transfers between devices  25.3 us (6%)
  other arithmetic  17.6 us (4%)
  between operations  14.5 us (3%)
  local copies, waits for them, and re-layouts  13.9 us (3%)
    all_to_all x1, waiting for transfers between devices, shards(): lax.all_to_all(jnp.stack([stacked] * lax.axis_size('seq')), 'seq', 0, 0)  122 us
    reduce_scatter x1, waiting for transfers between devices, shards(): lax.psum_scatter(partial_grad.astype(jnp.bfloat16), 'head', scatter_dimen...  92.5 us
    psum x1, waiting for transfers between devices, shards(): lax.psum(partial_value.astype(jnp.bfloat16), 'head').astype(jnp.float32)  87.2 us
    ppermute x4, waiting for transfers between devices, passed_along(): lax.ppermute(value, axis, [(source, source + steps) for source in range(l...  29 us
    ppermute x4, starting transfers between devices, passed_along(): lax.ppermute(value, axis, [(source, source + steps) for source in range(l...  13.7 us
    all_to_all x1, starting transfers between devices, shards(): lax.all_to_all(jnp.stack([stacked] * lax.axis_size('seq')), 'seq', 0, 0)  11.3 us
  transfers between devices with their start and end apart: 7, of which 7 were waited for; matrix products, arithmetic and copies ran while one was open for 2% of the time, Pallas kernels for 0%

profile of v1, /device:TPU:1, one launch (start us, length us, event | category | flops | bytes accessed | tf_op | source)
XLA Modules:
  0.0 438.6 jit_solution(2897041089497442286)
XLA Ops:
  8.2 2.8 stack.2
  11.0 11.3 %all-to-all-start = ((bf16[32,168,512]{2,1,0:T(8,128)(2,1)}), bf16[32,168,512]{2,1,0:T(8,128)(2,1)}, u32[]{:S(2)}, u32[]{:S(2)}) async-start(bf16[32,168,512]{2,1,0:T(8,128)(2,1)} %stack.2), calls=%async_computation | async-start | bytes 11010048 | tf_op jit(solution)/shard_map/all_to_all | solution.py:38
  22.7 122.1 %all-to-all-done = bf16[32,168,512]{2,1,0:T(8,128)(2,1)} async-done(((bf16[32,168,512]{2,1,0:T(8,128)(2,1)}), bf16[32,168,512]{2,1,0:T(8,128)(2,1)}, u32[]{:S(2)}, u32[]{:S(2)}) %all-to-all-start) | async-done | bytes 5505056 | tf_op jit(solution)/shard_map/all_to_all | solution.py:38
  144.8 6.8 %convolution_bitcast_fusion.2 = f32[512,512]{0,1:T(8,128)S(1)} fusion(bf16[5376,512]{1,0:T(8,128)(2,1)} %bitcast.1, bf16[512,5376]{1,0:T(8,128)(2,1)} %param.7), kind=kOutput, calls=%fused_computation.24 | convolution fusion | flops 2818572288 | bytes 12058624 | tf_op jit(solution)/shard_map/dot_general | solution.py:40
  154.2 2.5 collective-permute-start.1
  159.6 6.4 %collective-permute-done.1 = bf16[512,2,256]{2,0,1:T(8,128)(2,1)S(1)} collective-permute-done((bf16[512,2,256]{2,0,1:T(8,128)(2,1)S(1)}, bf16[512,2,256]{2,0,1:T(8,128)(2,1)S(1)}, u32[]{:S(2)}, u32[]{:S(2)}) %collective-permute-start.1) | collective-permute-done | bytes 524320 | tf_op jit(solution)/shard_map/ppermute | solution.py:16
  166.0 8.1 %collective-permute-done = bf16[512,2,256]{2,0,1:T(8,128)(2,1)S(1)} collective-permute-done((bf16[512,2,256]{2,0,1:T(8,128)(2,1)S(1)}, bf16[512,2,256]{2,0,1:T(8,128)(2,1)S(1)}, u32[]{:S(2)}, u32[]{:S(2)}) %collective-permute-start) | collective-permute-done | bytes 524320 | tf_op jit(solution)/shard_map/ppermute | solution.py:16
  174.2 3.3 fusion.2
  177.5 2.7 divide_convert_fusion
  180.2 1.8 copy-done.5
  182.1 2.6 copy-done.2
  187.3 87.2 %all-reduce.2.cloned.1.call-done = bf16[512,512]{1,0:T(8,128)(2,1)} async-done(((bf16[512,512]{1,0:T(8,128)(2,1)}), bf16[512,512]{1,0:T(8,128)(2,1)}) %all-reduce.2.cloned.1.call-update) | async-done | bytes 524304 | tf_op jit(solution)/shard_map/psum | solution.py:70
  276.1 2.3 convolution_convert_fusion.1
  278.4 1.8 convolution_bitcast_fusion
  280.2 6.9 %fusion = (f32[2,2,512]{2,1,0:T(2,128)S(1)}, f32[2,1536,512,2]{2,1,3,0:T(8,128)}) fusion(bf16[2,2,512,1536]{2,3,1,0:T(8,128)(2,1)S(1)} %copy-done.3, bf16[512,2,2,128]{0,3,2,1:T(8,128)(2,1)S(1)} %bitcast.88, bf16[1536,2,256]{2,0,1:T(8,128)(2,1)S(1)} %maximum_maximum_fusion), kind=kOutput, calls=%fused_computation.2 | convolution fusion | flops 814741504 | bytes 20193280 | tf_op jit(solution)/shard_map/qkgd,jkd->kgqj/dot_general | solution.py:85
  287.1 6.9 %fusion.1 = bf16[2,2,512,1536]{2,3,1,0:T(8,128)(2,1)S(1)} fusion(f32[2,1536,512,2]{2,1,3,0:T(8,128)} %get-tuple-element.11, f32[2,2,512]{2,1,0:T(2,128)S(1)} %get-tuple-element.10, f32[2,2,512]{2,1,0:T(2,128)S(1)} %get-tuple-element.8, f32[2,1536,512,2]{2,1,3,0:T(8,128)S(1)} %bitcast.86, pred[512,1536]{0,1:T(8,128)(4,1)S(1)} %copy-done.9), kind=kLoop, calls=%fused_computation.3 | loop fusion | flops 25165824 | bytes 32260096 | tf_op jit(solution)/shard_map/convert_element_type | solution.py:89
  294.1 1.8 fusion.7
  297.0 8.3 %collective-permute-start.2 = (bf16[512,2,256]{2,0,1:T(8,128)(2,1)S(1)}, bf16[512,2,256]{2,0,1:T(8,128)(2,1)S(1)}, u32[]{:S(2)}, u32[]{:S(2)}) collective-permute-start(bf16[512,2,256]{2,0,1:T(8,128)(2,1)S(1)} %get-tuple-element.6), channel_id=1, source_target_pairs={{8,0},{16,8},{24,16},{32,24},{40,32},{48,40},{56,48},{64,56},{72,6... | collective-permute-start | bytes 1572872 | tf_op jit(solution)/shard_map/ppermute | solution.py:16
  306.5 10.4 %collective-permute-done.2 = bf16[512,2,256]{2,0,1:T(8,128)(2,1)S(1)} collective-permute-done((bf16[512,2,256]{2,0,1:T(8,128)(2,1)S(1)}, bf16[512,2,256]{2,0,1:T(8,128)(2,1)S(1)}, u32[]{:S(2)}, u32[]{:S(2)}) %collective-permute-start.2) | collective-permute-done | bytes 524320 | tf_op jit(solution)/shard_map/ppermute | solution.py:16
  317.0 4.1 collective-permute-done.3
  324.0 7.4 %convolution_convert_fusion = bf16[512,5376]{0,1:T(8,128)(2,1)} fusion(bf16[5376,512]{1,0:T(8,128)(2,1)} %bitcast.1, bf16[512,256]{0,1:T(8,128)(2,1)S(1)} %bitcast.93, bf16[512,256]{0,1:T(8,128)(2,1)S(1)} %bitcast.94), kind=kOutput, calls=%fused_computation.8 | convolution fusion | flops 2822373376 | bytes 11534336 | tf_op jit(solution)/shard_map/dot_general | solution.py:121
  331.4 3.9 multiply_reduce_fusion
  336.9 92.5 %reduce-scatter.2.cloned.1.call-done = bf16[512,672]{0,1:T(8,128)(2,1)} async-done(((bf16[512,5376]{0,1:T(8,128)(2,1)}), bf16[512,672]{0,1:T(8,128)(2,1)}) %reduce-scatter.2.cloned.1.call-update) | async-done | bytes 688144 | tf_op jit(solution)/shard_map/reduce_scatter | solution.py:124
  429.4 2.4 convert_element_type.76
  (70 shorter events, 17.9 us)
Async XLA Ops:
  7.2 178.6 %copy-start = (bf16[512,512]{1,0:T(8,128)(2,1)S(1)}, bf16[512,512]{1,0:T(8,128)(2,1)}, u32[]{:S(2)}) copy-start(bf16[512,512]{1,0:T(8,128)(2,1)} %param.11) | copy-start | bytes 1572868
  11.0 11.4 %copy-start.10 = (bf16[512,512]{1,0:T(8,128)(2,1)S(1)}, bf16[512,512]{1,0:T(8,128)(2,1)}, u32[]{:S(2)}) copy-start(bf16[512,512]{1,0:T(8,128)(2,1)} %param.8) | copy-start | bytes 1572868
  11.0 133.9 %all-to-all-start = ((bf16[32,168,512]{2,1,0:T(8,128)(2,1)}), bf16[32,168,512]{2,1,0:T(8,128)(2,1)}, u32[]{:S(2)}, u32[]{:S(2)}) async-start(bf16[32,168,512]{2,1,0:T(8,128)(2,1)} %stack.2), calls=%async_computation | async-start | bytes 11010048 | tf_op jit(solution)/shard_map/all_to_all | solution.py:38
  22.3 252.2 %all-reduce.2.cloned.1.call-start = ((), (), s32[]{:S(2)}) async-start(), calls=%async_computation.2 | async-start | bytes 1048576 | tf_op jit(solution)/shard_map/psum | solution.py:70
  152.7 13.3 %copy-start.6 = (f32[512,2,128]{2,0,1:T(8,128)}, f32[512,2,128]{2,0,1:T(8,128)S(1)}, u32[]{:S(2)}) copy-start(f32[512,2,128]{2,0,1:T(8,128)S(1)} %copy.24) | copy-start | bytes 1572868
  154.2 11.7 %collective-permute-start.1 = (bf16[512,2,256]{2,0,1:T(8,128)(2,1)S(1)}, bf16[512,2,256]{2,0,1:T(8,128)(2,1)S(1)}, u32[]{:S(2)}, u32[]{:S(2)}) collective-permute-start(bf16[512,2,256]{2,0,1:T(8,128)(2,1)S(1)} %pad_maximum_fusion.1), channel_id=1, source_target_pairs={{0,8},{8,16},{16,24},{24,32},{32,40},{40,48},{48,56},{56,64},{64,7... | collective-permute-start | bytes 1572872 | tf_op jit(solution)/shard_map/ppermute | solution.py:16
  156.8 17.3 %collective-permute-start = (bf16[512,2,256]{2,0,1:T(8,128)(2,1)S(1)}, bf16[512,2,256]{2,0,1:T(8,128)(2,1)S(1)}, u32[]{:S(2)}, u32[]{:S(2)}) collective-permute-start(bf16[512,2,256]{2,0,1:T(8,128)(2,1)S(1)} %pad_maximum_fusion.1), channel_id=1, source_target_pairs={{0,16},{8,24},{16,32},{24,40},{32,48},{40,56},{48,64},{56,72},{64,... | collective-permute-start | bytes 1572872 | tf_op jit(solution)/shard_map/ppermute | solution.py:16
  159.6 17.9 %copy-start.8 = (pred[512,1536]{0,1:T(8,128)(4,1)}, pred[512,1536]{0,1:T(8,128)(4,1)S(1)}, u32[]{:S(2)}) copy-start(pred[512,1536]{0,1:T(8,128)(4,1)S(1)} %fusion.5) | copy-start | bytes 2359300
  177.5 4.5 %copy-start.5 = (f32[2,1536,512,2]{2,1,3,0:T(8,128)}, f32[2,1536,512,2]{2,1,3,0:T(8,128)S(1)}, u32[]{:S(2)}) copy-start(f32[2,1536,512,2]{2,1,3,0:T(8,128)S(1)} %get-tuple-element.9) | copy-start | bytes 37748740
  182.0 2.6 copy-start.2
  184.7 2.6 copy-start.11
  184.7 91.4 %copy-start.12 = (s32[512]{0:T(512)S(1)}, s32[512]{0:T(512)}, u32[]{:S(2)}) copy-start(s32[512]{0:T(512)} %param.13) | copy-start | bytes 6148
  187.0 242.4 %reduce-scatter.2.cloned.1.call-start = ((), (), s32[]{:S(2)}) async-start(), calls=%async_computation.3 | async-start | bytes 6193152 | tf_op jit(solution)/shard_map/reduce_scatter | solution.py:124
  274.5 3.9 copy-start.3
  278.4 8.7 %slice-start = ((s8[12582912]{0:T(1024)(128)(4,1)}), s8[4194304]{0:T(1024)(128)(4,1)S(1)}, s32[]{:S(2)}) async-start(s8[12582912]{0:T(1024)(128)(4,1)} %bitcast.85), calls=%async_computation.4 | async-start | bytes 8388608
  280.2 6.9 %slice-start.1 = ((s8[12582912]{0:T(1024)(128)(4,1)}), s8[4194304]{0:T(1024)(128)(4,1)S(1)}, s32[]{:S(2)}) async-start(s8[12582912]{0:T(1024)(128)(4,1)} %bitcast.85), calls=%async_computation.5 | async-start | bytes 8388608
  280.2 6.9 %slice-start.2 = ((s8[12582912]{0:T(1024)(128)(4,1)}), s8[4194304]{0:T(1024)(128)(4,1)S(1)}, s32[]{:S(2)}) async-start(s8[12582912]{0:T(1024)(128)(4,1)} %bitcast.85), calls=%async_computation.6 | async-start | bytes 8388608
  280.2 6.9 %copy-start.9 = (pred[512,1536]{0,1:T(8,128)(4,1)S(1)}, pred[512,1536]{0,1:T(8,128)(4,1)}, u32[]{:S(2)}) copy-start(pred[512,1536]{0,1:T(8,128)(4,1)} %copy-done.8) | copy-start | bytes 2359300
  294.0 2.7 copy-start.4
  296.7 24.5 %copy-start.7 = (f32[512,2,128]{2,0,1:T(8,128)S(1)}, f32[512,2,128]{2,0,1:T(8,128)}, u32[]{:S(2)}) copy-start(f32[512,2,128]{2,0,1:T(8,128)} %copy-done.6) | copy-start | bytes 1572868
  297.0 20.0 %collective-permute-start.2 = (bf16[512,2,256]{2,0,1:T(8,128)(2,1)S(1)}, bf16[512,2,256]{2,0,1:T(8,128)(2,1)S(1)}, u32[]{:S(2)}, u32[]{:S(2)}) collective-permute-start(bf16[512,2,256]{2,0,1:T(8,128)(2,1)S(1)} %get-tuple-element.6), channel_id=1, source_target_pairs={{8,0},{16,8},{24,16},{32,24},{40,32},{48,40},{56,48},{64,56},{72,6... | collective-permute-start | bytes 1572872 | tf_op jit(solution)/shard_map/ppermute | solution.py:16
  305.2 15.8 %collective-permute-start.3 = (bf16[512,2,256]{2,0,1:T(8,128)(2,1)S(1)}, bf16[512,2,256]{2,0,1:T(8,128)(2,1)S(1)}, u32[]{:S(2)}, u32[]{:S(2)}) collective-permute-start(bf16[512,2,256]{2,0,1:T(8,128)(2,1)S(1)} %get-tuple-element.7), channel_id=1, source_target_pairs={{16,0},{24,8},{32,16},{40,24},{48,32},{56,40},{64,48},{72,56},{80,... | collective-permute-start | bytes 1572872 | tf_op jit(solution)/shard_map/ppermute | solution.py:16
  331.4 100.3 %copy-start.1 = (bf16[512,512]{1,0:T(8,128)(2,1)S(1)}, bf16[512,512]{1,0:T(8,128)(2,1)}, u32[]{:S(2)}) copy-start(bf16[512,512]{1,0:T(8,128)(2,1)} %param.11) | copy-start | bytes 1572868
Sparse Core Ops, SparseCore 0:
  187.1 87.3 all-reduce.1
  331.5 97.8 reduce-scatter.1
